TPU v7x, 32 devices: a whole 2x2x4 slice. The times are simulated.
32 devices in a mesh: layer: 4 (over x, core), dp: 8 (over z, y).
Axes of the slice: x: 2, y: 2, z: 4, core: 2. Of those that a mesh axis runs over, the one named last changes fastest.
Arguments:
- out_grads: bfloat16 [4, 128, 16384], P('layer', None, 'dp'), may hold values from -3 to 3
- in_acts: bfloat16 [4, 128, 4096], P('layer', None, 'dp'), may hold values from -3 to 3
- out_basis: bfloat16 [4, 16384, 16384], P('layer', None, 'dp'), may hold values from -0.046875 to 0.046875
- in_basis: bfloat16 [4, 4096, 4096], P('layer', None, 'dp'), may hold values from -0.09375 to 0.09375
- eigenvalues: bfloat16 [4, 16384, 4096], P('layer', 'dp'), may hold values from 0.5 to 50
- out_store: bfloat16 [4, 16, 32, 16384], P('layer', 'dp'), may hold values from -0.046875 to 0.046875
- in_store: bfloat16 [4, 16, 32, 4096], P('layer', 'dp'), may hold values from -0.09375 to 0.09375
- counts: int32 [16], P('dp'), may hold values from 1 to 4096
- winners: int32 [4, 6], replicated, may hold values from 0 to 15
Outputs:
- influence: float32 [4, 6, 32], replicated
All inputs are finite; a program needn't handle non-finite values.
Results may differ from a plain program's by a relative error of at most 0.0055.
Values may be sent and summed in bfloat16 or wider, within the bound.
A program may use at most 192 MiB of HBM per device.

v0:
```python
import jax
import jax.numpy as jnp
from jax import lax
from jax.sharding import PartitionSpec as P

NQ = 4
TQ = 32
WIN = 6
R = 32
SPAN = 128


damping = 0.1


def on_device(
    out_grads, in_acts, out_basis, in_basis, eigenvalues, out_store, in_store, counts, winners
):
    out_local = out_basis[0]
    in_local = in_basis[0]
    out_width = out_local.shape[1]
    rows = out_local
    turned_out = jnp.dot(
        lax.all_gather(out_grads[0], "dp", axis=1, tiled=True),
        rows,
        preferred_element_type=jnp.float32,
    ).astype(jnp.bfloat16)
    rows = in_local
    turned_part = jnp.dot(
        lax.all_gather(in_acts[0], "dp", axis=1, tiled=True),
        rows,
        preferred_element_type=jnp.float32,
    ).astype(jnp.bfloat16)
    turned_in = lax.all_gather(turned_part, "dp", axis=1, tiled=True)
    left = turned_out.reshape(NQ, TQ, out_width)
    right = turned_in.reshape(NQ, TQ, turned_in.shape[1])
    product = jnp.einsum("qtf,qtd->qfd", left, right, preferred_element_type=jnp.float32)
    divisor = eigenvalues[0].astype(jnp.float32) + damping
    precond = (product / divisor[None]).astype(jnp.bfloat16)
    alive = (jnp.arange(R, dtype=jnp.int32)[None, :] * SPAN < counts[:, None]).astype(jnp.bfloat16)
    masked = in_store[0] * alive[:, :, None]
    out_slices = lax.all_to_all(out_store[0], "dp", split_axis=2, concat_axis=0, tiled=True)
    chosen = winners.reshape(NQ * WIN)
    left_rows = jnp.take(out_slices, chosen, axis=0).reshape(NQ, WIN * R, out_width)
    full_width = turned_in.shape[1]
    in_whole = lax.all_gather(masked, "dp", axis=0, tiled=True)
    right_rows = jnp.take(in_whole, chosen, axis=0).reshape(NQ, WIN * R, full_width)
    mapped = jnp.einsum("qfd,qkd->qkf", precond, right_rows, preferred_element_type=jnp.float32)
    partial_value = jnp.sum(mapped * left_rows.astype(jnp.float32), axis=2)
    totals = lax.psum(partial_value, ("layer", "dp"))
    return totals.reshape(NQ, WIN, R)


def solution(mesh):
    placed = (
        P("layer", None, "dp"),
        P("layer", None, "dp"),
        P("layer", None, "dp"),
        P("layer", None, "dp"),
        P("layer", "dp", None),
        P("layer", "dp", None, None),
        P("layer", "dp", None, None),
        P("dp"),
        P(),
    )
    return jax.shard_map(on_device, mesh=mesh, in_specs=placed, out_specs=P(), check_vma=False)
```

profile of v0, /device:TPU:0, one launch (start us, length us, event | category | flops | bytes accessed | tf_op | source)
XLA Modules:
  0.0 364.3 jit_solution(16281501123913025915)
XLA Ops:
  6.5 0.7 all-gather.13.cloned.1.call-update
  7.3 0.0 all-gather.11.cloned.1.call-start
  7.3 0.7 all-gather.11.cloned.1.call-update
  8.0 0.0 all-gather.7.cloned.1.call-start
  8.1 0.7 compare_convert_fusion
  8.8 2.0 bitcast_multiply_fusion
  10.7 0.0 all-gather.7.cloned.1.call-update
  10.8 17.2 %copy.13 = bf16[1,2,32,16384]{2,1,3,0:T(2,128)(2,1)} copy(bf16[1,2,32,16384]{3,2,1,0:T(8,128)(2,1)} %param.14) | data formatting | bytes 4194304 | tf_op args[5]
  28.0 8.0 %bitcast_bitcast_fusion = bf16[16384,2,32]{2,1,0:T(2,128)(2,1)} fusion(bf16[1,2,32,16384]{2,1,3,0:T(2,128)(2,1)} %copy.13), kind=kLoop, calls=%fused_computation.25 | loop fusion | bytes 4194304
  36.0 11.2 %reshape.112 = bf16[8,2,65536]{2,1,0:T(2,128)(2,1)} reshape(bf16[16384,2,32]{2,1,0:T(2,128)(2,1)} %bitcast_bitcast_fusion) | data formatting | bytes 4194304
  47.2 7.3 %all-to-all-start = ((bf16[8,2,65536]{2,1,0:T(2,128)(2,1)}), bf16[8,2,65536]{2,1,0:T(2,128)(2,1)S(1)}, u32[]{:S(2)}, u32[]{:S(2)}) async-start(bf16[8,2,65536]{2,1,0:T(2,128)(2,1)} %reshape.112), calls=%async_computation | async-start | bytes 4194304 | tf_op jit(solution)/shard_map/all_to_all | solution.py:42
  54.5 0.0 all-gather.9.cloned.1.call-start
  54.6 0.1 reshape.90
  54.7 0.1 broadcast_in_dim.28
  54.8 0.1 broadcast_in_dim.29
  54.9 18.8 %add_bitcast_fusion = f32[2048,4096]{1,0:T(8,128)} fusion(bf16[1,2048,4096]{2,1,0:T(8,128)(2,1)} %param.13), kind=kLoop, calls=%fused_computation.6 | loop fusion | flops 16777216 | bytes 50331648 | tf_op jit(solution)/shard_map/div | solution.py:39
  73.7 3.9 %fusion.13 = bf16[128,512]{1,0:T(8,128)(2,1)} fusion(bf16[1,4096,512]{2,1,0:T(8,128)(2,1)} %param.12, bf16[1,128,4096]{2,1,0:T(8,128)(2,1)} %all-gather.13.cloned.1.call-done), kind=kOutput, calls=%fused_computation.15 | convolution fusion | flops 536936448 | bytes 5373952 | tf_op jit(solution)/shard_map/dot_general | solution.py:29
  77.6 0.0 all-gather.9.cloned.1.call-update
  77.6 50.9 %all-to-all-done = bf16[8,2,65536]{2,1,0:T(2,128)(2,1)S(1)} async-done(((bf16[8,2,65536]{2,1,0:T(2,128)(2,1)}), bf16[8,2,65536]{2,1,0:T(2,128)(2,1)S(1)}, u32[]{:S(2)}, u32[]{:S(2)}) %all-to-all-start) | async-done | bytes 2097184 | tf_op jit(solution)/shard_map/all_to_all | solution.py:42
  128.5 6.5 %reshape.113 = bf16[16384,2,32]{2,1,0:T(2,128)(2,1)} reshape(bf16[8,2,65536]{2,1,0:T(2,128)(2,1)S(1)} %all-to-all-done) | data formatting | bytes 4194304
  135.0 17.8 %copy.18 = bf16[2,32,8,2048]{3,1,0,2:T(8,128)(2,1)S(1)} copy(bf16[2,32,8,2048]{1,0,3,2:T(2,128)(2,1)} %bitcast.47) | data formatting | bytes 4194304 | tf_op jit(solution)/shard_map/all_to_all | solution.py:42
  152.8 2.5 gather_fusion.1
  155.3 26.3 %fusion.8 = bf16[128,2048]{1,0:T(8,128)(2,1)} fusion(bf16[1,16384,2048]{2,1,0:T(8,128)(2,1)} %param.11, bf16[1,128,16384]{2,1,0:T(8,128)(2,1)} %all-gather.11.cloned.1.call-done), kind=kOutput, calls=%fused_computation.14 | convolution fusion | flops 8590196736 | bytes 71827456 | tf_op jit(solution)/shard_map/dot_general | solution.py:23
  181.5 46.3 %all-gather.7.cloned.1.call-done = bf16[16,32,4096]{2,1,0:T(8,128)(2,1)} async-done(((bf16[2,32,4096]{2,1,0:T(8,128)(2,1)}), bf16[16,32,4096]{2,1,0:T(8,128)(2,1)}) %all-gather.7.cloned.1.call-update) | async-done | bytes 4194320 | tf_op jit(solution)/shard_map/all_gather | solution.py:46
  227.8 6.5 %gather_fusion = bf16[24,32,4096]{2,1,0:T(8,128)(2,1)} fusion(bf16[16,32,4096]{2,1,0:T(8,128)(2,1)} %all-gather.7.cloned.1.call-done, s32[1024]{0:T(1024)S(1)} %pad_clamp_fusion), kind=kCustom, calls=%fused_computation | custom fusion | bytes 12583008 | tf_op jit(solution)/shard_map/jit(_take)/gather | solution.py:47
  234.3 6.2 %bitcast_select_fusion = bf16[4,192,4096]{2,1,0:T(8,128)(2,1)} fusion(pred[4,192]{1,0:T(4,128)(4,1)S(1)} %broadcast_in_dim.29, bf16[4,192,4096]{2,1,0:T(8,128)(2,1)} %bitcast.48), kind=kLoop, calls=%fused_computation.8 | loop fusion | flops 3145728 | bytes 12583680 | tf_op jit(solution)/shard_map/jit(_take)/select_n | solution.py:47
  240.5 27.2 %all-gather.9.cloned.1.call-done = bf16[128,4096]{1,0:T(8,128)(2,1)} async-done(((bf16[128,512]{1,0:T(8,128)(2,1)}), bf16[128,4096]{1,0:T(8,128)(2,1)}) %all-gather.9.cloned.1.call-update) | async-done | bytes 1048592 | tf_op jit(solution)/shard_map/all_gather | solution.py:34
  267.7 45.8 %fusion.2 = f32[4,192,2048]{2,1,0:T(8,128)} fusion(bf16[4,192,4096]{2,1,0:T(8,128)(2,1)} %bitcast_select_fusion, f32[2048,4096]{1,0:T(8,128)} %add_bitcast_fusion, bf16[4,32,2048]{2,1,0:T(8,128)(2,1)} %bitcast.51, bf16[4,32,4096]{2,1,0:T(8,128)(2,1)} %bitcast.52), kind=kOutput, calls=%fused_computation.5 | convolution fusion | flops 15099494400 | bytes 47710208 | tf_op jit(solution)/shard_map/qfd,qkd->qkf/dot_general | solution.py:48
  313.5 3.8 %multiply_reduce_fusion = f32[4,192]{1,0:T(4,128)S(1)} fusion(f32[4,192,2048]{2,1,0:T(8,128)} %fusion.2, pred[4,192]{1,0:T(4,128)(4,1)S(1)} %broadcast_in_dim.29, bf16[4,192,2048]{2,1,0:T(8,128)(2,1)S(1)} %bitcast.50), kind=kLoop, calls=%fused_computation.9 | loop fusion | flops 6290688 | bytes 9441024 | tf_op jit(solution)/shard_map/reduce_sum | solution.py:49
  317.3 0.1 reshape.93
  317.4 39.8 %psum.7 = f32[4,6,32]{2,1,0:T(8,128)S(1)} all-reduce(f32[4,6,32]{2,1,0:T(8,128)S(1)} %reshape.93), channel_id=1, replica_groups=mesh['layer'=4,'dp'=8] {'layer','dp'}, use_global_device_ids=true, to_apply=%region_1.2 | all-reduce | flops 768 | bytes 6144 | tf_op jit(solution)/shard_map/psum | solution.py:50
  357.2 0.6 copy.16
  (11 shorter events, 0.0 us)
Async XLA Ops:
  6.5 67.1 %all-gather.13.cloned.1.call-start = ((), (), s32[]{:S(2)}) async-start(), calls=%async_computation.4 | async-start | bytes 1179648 | tf_op jit(solution)/shard_map/all_gather | solution.py:30
  7.3 148.0 %all-gather.11.cloned.1.call-start = ((), (), s32[]{:S(2)}) async-start(), calls=%async_computation.3 | async-start | bytes 4718592 | tf_op jit(solution)/shard_map/all_gather | solution.py:24
  8.0 219.8 %all-gather.7.cloned.1.call-start = ((), (), s32[]{:S(2)}) async-start(), calls=%async_computation.1 | async-start | bytes 4718592 | tf_op jit(solution)/shard_map/all_gather | solution.py:46
  36.0 18.6 %copy-start.1 = (s32[4,6]{1,0:T(4,128)S(1)}, s32[4,6]{1,0:T(4,128)}, u32[]{:S(2)}) copy-start(s32[4,6]{1,0:T(4,128)} %param.17) | copy-start | bytes 292
  47.2 81.3 %all-to-all-start = ((bf16[8,2,65536]{2,1,0:T(2,128)(2,1)}), bf16[8,2,65536]{2,1,0:T(2,128)(2,1)S(1)}, u32[]{:S(2)}, u32[]{:S(2)}) async-start(bf16[8,2,65536]{2,1,0:T(2,128)(2,1)} %reshape.112), calls=%async_computation | async-start | bytes 4194304 | tf_op jit(solution)/shard_map/all_to_all | solution.py:42
  54.5 213.1 %all-gather.9.cloned.1.call-start = ((), (), s32[]{:S(2)}) async-start(), calls=%async_computation.2 | async-start | bytes 1179648 | tf_op jit(solution)/shard_map/all_gather | solution.py:34
  267.7 45.8 %copy-start = (bf16[24,32,2048]{2,1,0:T(8,128)(2,1)S(1)}, bf16[24,32,2048]{2,1,0:T(8,128)(2,1)}, u32[]{:S(2)}) copy-start(bf16[24,32,2048]{2,1,0:T(8,128)(2,1)} %gather_fusion.1) | copy-start | bytes 9437188
Sparse Core Ops, SparseCore 0:
  9.4 42.1 all-gather.12
  53.7 100.1 all-gather.10
  156.0 71.7 all-gather.6
  229.7 37.9 all-gather.8
where the time goes:
time: 366 us; the launch traced here: 364 us
  waiting for transfers between devices  126 us (34%)
  matrix products  76 us (21%)
  local copies, waits for them, and re-layouts  70.7 us (19%)
  blocking collectives  39.8 us (11%)
  other arithmetic  31.4 us (9%)
  between operations  13.2 us (4%)
  starting transfers between devices  7.43 us (2%)
    all_to_all x1, waiting for transfers between devices, on_device(): lax.all_to_all(out_store[0], 'dp', split_axis=2, concat_axis=0, tiled=True)  50.9 us
    all_gather x1, waiting for transfers between devices, on_device(): in_whole = lax.all_gather(masked, 'dp', axis=0, tiled=True)  46.3 us
    dot_general x1, matrix products, on_device(): jnp.einsum('qfd,qkd->qkf', precond, right_rows, preferred_element_type=jn...  45.8 us
    unnamed x8, local copies, waits for them, and re-layouts  43 us
    psum x1, blocking collectives, on_device(): totals = lax.psum(partial_value, ('layer', 'dp'))  39.8 us
    all_gather x1, waiting for transfers between devices, on_device(): turned_in = lax.all_gather(turned_part, 'dp', axis=1, tiled=True)  27.2 us
    dot_general x1, matrix products, on_device(): jnp.dot(lax.all_gather(out_grads[0], 'dp', axis=1, tiled=True), rows, pre...  26.3 us
    div x1, other arithmetic, on_device(): precond = (product / divisor[None]).astype(jnp.bfloat16)  18.8 us
  transfers between devices with their start and end apart: 5, of which 3 were waited for; matrix products, arithmetic and copies ran while one was open for 35% of the time, Pallas kernels for 0%

commit v1 on v0

v1 whole, which is shorter than its diff:
```python
import functools

import jax
import jax.numpy as jnp
from jax import lax
from jax.experimental import pallas as pl
from jax.experimental.pallas import tpu as pltpu
from jax.sharding import PartitionSpec as P

NQ = 4
TQ = 32
WIN = 6
R = 32
SPAN = 128
COLS = 256
BUFFERS = 3
MESH = pl.DeviceIdType.MESH


damping = 0.1


class Gather:
    def __init__(self, n, me, own, full, send_sem, recv_sem):
        self.n, self.nh = n, n // 2
        self.h, self.y = me // 2, lax.rem(me, 2)
        self.own, self.full, self.send_sem, self.recv_sem = own, full, send_sem, recv_sem
        self.half = full.shape[1] // 2
        small = (self.nh - 1) // 2
        large = self.nh - 1 - small
        self.reach = (((-1, small), (1, large)), ((-1, large), (1, small)))
        self.waves = large
        self.pending = []

    def index(self, dh, other):
        return lax.rem(self.h + dh + self.nh, self.nh) * 2 + (1 - self.y if other else self.y)

    def place(self, ref, part):
        return ref.at[pl.ds(part * self.half, self.half)]

    def send(self, part, dh, way):
        j = self.index(dh, False)
        if way == 0:
            to, slot = self.index(0, True), 2
        else:
            to, slot = self.index(way, False), (way + 1) // 2
        target = self.place(self.full.at[j], part)
        source = self.place(self.own, part) if dh == 0 else target
        copy = pltpu.make_async_remote_copy(
            src_ref=source,
            dst_ref=target,
            send_sem=self.send_sem.at[part, dh + self.nh, slot],
            recv_sem=self.recv_sem.at[part, j],
            device_id={"dp": to},
            device_id_type=MESH,
        )
        copy.start()
        self.pending.append(copy)

    def wait(self, part, dh, other):
        j = self.index(dh, other)
        target = self.place(self.full.at[j], part)
        pltpu.make_async_remote_copy(
            src_ref=target,
            dst_ref=target,
            send_sem=self.send_sem.at[part, 0, 0],
            recv_sem=self.recv_sem.at[part, j],
            device_id={"dp": self.index(0, True)},
            device_id_type=MESH,
        ).wait_recv()

    def start(self):
        for part in (0, 1):
            for way, reach in self.reach[part]:
                if reach > 0:
                    self.send(part, 0, way)
            self.send(part, 0, 0)

    def wave(self, w):
        for part in (0, 1):
            for way, reach in self.reach[part]:
                if w <= reach:
                    dh = -way * w
                    self.wait(part, dh, False)
                    if w < reach:
                        self.send(part, dh, way)
                    self.send(part, dh, 0)

    def finish(self):
        for part in (0, 1):
            self.wait(part, 0, True)
        for w in range(1, self.waves + 1):
            for part in (0, 1):
                for way, reach in self.reach[part]:
                    if w <= reach:
                        self.wait(part, -way * w, True)

    def drain(self):
        for copy in self.pending:
            copy.wait_send()


def rotate_kernel(
    n,
    og_ref,
    ia_ref,
    mk_ref,
    os_ref,
    ob_ref,
    ib_ref,
    to_ref,
    ti_ref,
    mk_all,
    os_all,
    og_all,
    ia_all,
    ti_own,
    ib_buf,
    ob_buf,
    acc,
    local_sem,
    ob_sem,
    og_send,
    og_recv,
    ia_send,
    ia_recv,
    mk_send,
    mk_recv,
    ti_send,
    ti_recv,
    os_send,
    os_recv,
):
    me = lax.axis_index("dp")
    nh = n // 2
    h, y = me // 2, lax.rem(me, 2)
    depth = og_ref.shape[1]
    width = ob_ref.shape[1]
    in_depth = ia_ref.shape[1]

    def chunk_index(k):
        return lax.rem(h + lax.rem(k, nh), nh) * 2 + lax.rem(y + k // nh, 2)

    def fetch(k, slot):
        rows = pl.ds(pl.multiple_of(chunk_index(k) * depth, depth), depth)
        return pltpu.make_async_copy(ob_ref.at[rows], ob_buf.at[slot], ob_sem.at[slot])

    locals_ = [
        pltpu.make_async_copy(ia_ref, ia_all.at[me], local_sem.at[0]),
        pltpu.make_async_copy(og_ref, og_all.at[me], local_sem.at[1]),
        pltpu.make_async_copy(ib_ref, ib_buf, local_sem.at[2]),
        pltpu.make_async_copy(mk_ref, mk_all.at[me], local_sem.at[3]),
        pltpu.make_async_copy(
            os_ref.at[:, pl.ds(pl.multiple_of(me * width, width), width)],
            os_all.at[me],
            local_sem.at[4],
        ),
    ]
    for copy in locals_:
        copy.start()
    for k in range(min(BUFFERS, n)):
        fetch(k, k).start()

    barrier = pltpu.get_barrier_semaphore()

    @pl.loop(1, n)
    def _(d):
        pl.semaphore_signal(
            barrier, inc=1, device_id={"dp": lax.rem(me + d, n)}, device_id_type=MESH
        )

    pl.semaphore_wait(barrier, n - 1)

    ia = Gather(n, me, ia_ref, ia_all, ia_send, ia_recv)
    og = Gather(n, me, og_ref, og_all, og_send, og_recv)
    mk = Gather(n, me, mk_ref, mk_all, mk_send, mk_recv)
    ti = Gather(n, me, ti_own, ti_ref, ti_send, ti_recv)

    def slices(d):
        to = lax.rem(me + d, n)
        return pltpu.make_async_remote_copy(
            src_ref=os_ref.at[:, pl.ds(pl.multiple_of(to * width, width), width)],
            dst_ref=os_all.at[me],
            send_sem=os_send.at[d],
            recv_sem=os_recv.at[me],
            device_id={"dp": to},
            device_id_type=MESH,
        )

    def dots(low, high):
        def one(k, carry):
            slot = lax.rem(k, BUFFERS)
            fetch(k, slot).wait()
            j = chunk_index(k)

            @pl.loop(0, width // COLS)
            def _(c):
                cols = pl.ds(pl.multiple_of(c * COLS, COLS), COLS)
                acc[:, cols] += jnp.dot(
                    og_all[j], ob_buf[slot, :, cols], preferred_element_type=jnp.float32
                )

            @pl.when(k + BUFFERS < n)
            def _():
                fetch(k + BUFFERS, slot).start()

            return carry

        lax.fori_loop(low, high, one, 0)

    ia.start()
    og.start()
    acc[...] = jnp.zeros_like(acc)
    for copy in locals_:
        copy.wait()
    for w in range(1, ia.waves + 1):
        ia.wave(w)
    ia.finish()
    og.wave(1)
    mk.start()

    def rotate(j, total):
        rows = pl.ds(pl.multiple_of(j * in_depth, in_depth), in_depth)
        return total + jnp.dot(ia_all[j], ib_buf[rows, :], preferred_element_type=jnp.float32)

    total = lax.fori_loop(0, n, rotate, jnp.zeros((ia_ref.shape[0], ib_ref.shape[1]), jnp.float32))
    ti_own[...] = total.astype(ti_own.dtype)
    own_turned = pltpu.make_async_copy(ti_own, ti_ref.at[me], local_sem.at[5])
    own_turned.start()
    ti.start()
    for w in range(2, og.waves + 1):
        og.wave(w)
    dots(0, 1)
    og.finish()
    mk.wave(1)
    ti.wave(1)
    dots(1, nh)
    for w in range(2, mk.waves + 1):
        mk.wave(w)
        ti.wave(w)

    @pl.loop(1, n)
    def _(d):
        slices(d).start()

    dots(nh, n)
    to_ref[...] = acc[...].astype(to_ref.dtype)
    mk.finish()
    ti.finish()
    own_turned.wait()
    for gather in (ia, og, mk, ti):
        gather.drain()

    @pl.loop(1, n)
    def _(d):
        slices(d).wait_send()
        source = lax.rem(me + d, n)
        pltpu.make_async_remote_copy(
            src_ref=os_all.at[source],
            dst_ref=os_all.at[source],
            send_sem=os_send.at[0],
            recv_sem=os_recv.at[source],
            device_id={"dp": source},
            device_id_type=MESH,
        ).wait_recv()


def rotate(n, og, ia, mk, out_store, out_basis, in_basis):
    tokens, depth = og.shape
    in_depth = ia.shape[1]
    width, in_width = out_basis.shape[1], in_basis.shape[1]
    rows, full = mk.shape
    nh = n // 2
    sends = pltpu.SemaphoreType.DMA((2, 2 * nh, 3))
    recvs = pltpu.SemaphoreType.DMA((2, n))
    dtype = og.dtype
    anywhere = pl.BlockSpec(memory_space=pl.ANY)
    vmem = pl.BlockSpec(memory_space=pltpu.VMEM)
    return pl.pallas_call(
        functools.partial(rotate_kernel, n),
        out_shape=(
            jax.ShapeDtypeStruct((tokens, width), dtype),
            jax.ShapeDtypeStruct((n, tokens, in_width), dtype),
            jax.ShapeDtypeStruct((n, rows, full), dtype),
            jax.ShapeDtypeStruct((n, rows, width), dtype),
        ),
        in_specs=[anywhere] * 6,
        out_specs=(vmem,) * 4,
        scratch_shapes=[
            pltpu.VMEM((n, tokens, depth), dtype),
            pltpu.VMEM((n, tokens, in_depth), dtype),
            pltpu.VMEM((tokens, in_width), dtype),
            pltpu.VMEM(in_basis.shape, dtype),
            pltpu.VMEM((BUFFERS, depth, width), dtype),
            pltpu.VMEM((tokens, width), jnp.float32),
            pltpu.SemaphoreType.DMA((6,)),
            pltpu.SemaphoreType.DMA((BUFFERS,)),
            sends,
            recvs,
            sends,
            recvs,
            sends,
            recvs,
            sends,
            recvs,
            pltpu.SemaphoreType.DMA((n,)),
            pltpu.SemaphoreType.DMA((n,)),
        ],
        compiler_params=pltpu.CompilerParams(
            collective_id=0, has_side_effects=True, vmem_limit_bytes=60 << 20
        ),
    )(og, ia, mk, out_store, out_basis, in_basis)


def total_kernel(n, layers, x_ref, out_ref, dp_slots, sub_total, layer_slots, local_sem, dp_send, dp_recv, layer_send, layer_recv):
    me, my_layer = lax.axis_index("dp"), lax.axis_index("layer")
    barrier = pltpu.get_barrier_semaphore()
    for axis, size, at in (("dp", n, me), ("layer", layers, my_layer)):

        @pl.loop(1, size)
        def _(d):
            pl.semaphore_signal(
                barrier, inc=1, device_id={axis: lax.rem(at + d, size)}, device_id_type=MESH
            )

    pl.semaphore_wait(barrier, n + layers - 2)

    def stage(axis, size, at, source, slots, send_sem, recv_sem):
        own = pltpu.make_async_copy(source, slots.at[at], local_sem)
        own.start()

        def push(d, slot):
            return pltpu.make_async_remote_copy(
                src_ref=source,
                dst_ref=slots.at[slot],
                send_sem=send_sem.at[d],
                recv_sem=recv_sem.at[slot],
                device_id={axis: lax.rem(at + d, size)},
                device_id_type=MESH,
            )

        @pl.loop(1, size)
        def _(d):
            push(d, at).start()

        own.wait()

        @pl.loop(1, size)
        def _(d):
            push(d, lax.rem(at + d, size)).wait()

        return lax.fori_loop(
            0, size, lambda i, total: total + slots[i], jnp.zeros(slots.shape[1:], slots.dtype)
        )

    sub_total[...] = stage("dp", n, me, x_ref, dp_slots, dp_send, dp_recv)
    out_ref[...] = stage("layer", layers, my_layer, sub_total, layer_slots, layer_send, layer_recv)


def total(n, layers, x):
    vmem = pl.BlockSpec(memory_space=pltpu.VMEM)
    return pl.pallas_call(
        functools.partial(total_kernel, n, layers),
        out_shape=jax.ShapeDtypeStruct(x.shape, x.dtype),
        in_specs=[vmem],
        out_specs=vmem,
        scratch_shapes=[
            pltpu.VMEM((n, *x.shape), x.dtype),
            pltpu.VMEM(x.shape, x.dtype),
            pltpu.VMEM((layers, *x.shape), x.dtype),
            pltpu.SemaphoreType.DMA,
            pltpu.SemaphoreType.DMA((n,)),
            pltpu.SemaphoreType.DMA((n,)),
            pltpu.SemaphoreType.DMA((layers,)),
            pltpu.SemaphoreType.DMA((layers,)),
        ],
        compiler_params=pltpu.CompilerParams(
            collective_id=1, has_side_effects=True, vmem_limit_bytes=8 << 20
        ),
    )(x)


def on_device(
    n, layers,
    out_grads, in_acts, out_basis, in_basis, eigenvalues, out_store, in_store, counts, winners
):
    _, seqs, tokens, features = in_store.shape
    width = out_basis.shape[2]
    alive = (jnp.arange(R, dtype=jnp.int32)[None, :] * SPAN < counts[:, None]).astype(jnp.bfloat16)
    masked = in_store[0] * alive[:, :, None]
    turned_out, turned_in, in_whole, out_slices = rotate(
        n,
        out_grads[0],
        in_acts[0],
        masked.reshape(seqs * tokens, features),
        out_store[0].reshape(seqs * tokens, out_store.shape[3]),
        out_basis[0],
        in_basis[0],
    )
    in_whole = in_whole.reshape(n * seqs, tokens, features)
    out_slices = out_slices.reshape(n * seqs, tokens, width)
    left = turned_out.reshape(NQ, TQ, width)
    right = turned_in.reshape(n, NQ, TQ, in_basis.shape[2]).transpose(1, 2, 0, 3).reshape(NQ, TQ, features)
    product = jnp.einsum("qtf,qtd->qfd", left, right, preferred_element_type=jnp.float32)
    divisor = eigenvalues[0].astype(jnp.float32) + damping
    precond = (product / divisor[None]).astype(jnp.bfloat16)
    chosen = winners.reshape(NQ * WIN)
    left_rows = jnp.take(out_slices, chosen, axis=0).reshape(NQ, WIN * R, width)
    right_rows = jnp.take(in_whole, chosen, axis=0).reshape(NQ, WIN * R, features)
    mapped = jnp.einsum("qfd,qkd->qkf", precond, right_rows, preferred_element_type=jnp.float32)
    partial_value = jnp.sum(mapped * left_rows.astype(jnp.float32), axis=2)
    return total(n, layers, partial_value).reshape(NQ, WIN, R)


def solution(mesh):
    placed = (
        P("layer", None, "dp"),
        P("layer", None, "dp"),
        P("layer", None, "dp"),
        P("layer", None, "dp"),
        P("layer", "dp", None),
        P("layer", "dp", None, None),
        P("layer", "dp", None, None),
        P("dp"),
        P(),
    )
    body = functools.partial(on_device, mesh.shape["dp"], mesh.shape["layer"])
    return jax.shard_map(body, mesh=mesh, in_specs=placed, out_specs=P(), check_vma=False)
```

time: 366 us -> 259 us (0.71)
  Pallas kernels: 0 us -> 170 us
  waiting for transfers between devices: 126 us -> 0 us
  local copies, waits for them, and re-layouts: 70.7 us -> 12.1 us
  blocking collectives: 39.8 us -> 0 us
  matrix products: 76 us -> 45.9 us
  between operations: 13.2 us -> 0.08 us
  starting transfers between devices: 7.43 us -> 0 us
    pallas_call x0 -> x2, Pallas kernels: none -> 170 us  [the longest x1 160 us: rotate(): pl.pallas_call(functools.partial(rotate_kernel, n), out_shape=(jax.ShapeD...]
    all_gather x4 -> x0, waiting for transfers between devices: 73.5 us -> none  [the longest x1 46.3 us: on_device(): in_whole = lax.all_gather(masked, 'dp', axis=0, tiled=True)]
    all_to_all x1 -> x0, waiting for transfers between devices: 50.9 us -> none  [on_device(): lax.all_to_all(out_store[0], 'dp', split_axis=2, concat_axis=0, tiled=True)]
    unnamed x8 -> x12, local copies, waits for them, and re-layouts: 43 us -> 0.02 us
    psum x1 -> x0, blocking collectives: 39.8 us -> none  [on_device(): totals = lax.psum(partial_value, ('layer', 'dp'))]
    dot_general x2 -> x0, matrix products: 30.2 us -> none  [the longest x1 26.3 us: on_device(): jnp.dot(lax.all_gather(out_grads[0], 'dp', axis=1, tiled=True), rows, pre...]
    all_to_all x1 -> x0, local copies, waits for them, and re-layouts: 17.8 us -> none  [on_device(): lax.all_to_all(out_store[0], 'dp', split_axis=2, concat_axis=0, tiled=True)]
    all_to_all x1 -> x0, starting transfers between devices: 7.32 us -> none  [on_device(): lax.all_to_all(out_store[0], 'dp', split_axis=2, concat_axis=0, tiled=True)]
  transfers between devices with their start and end apart: 5 -> 0, of which waited for: 3 -> 0; matrix products, arithmetic and copies ran while one was open for 35% -> 0% of each run, Pallas kernels for 0% -> 0%
where the time goes in v1:
time: 259 us; the launch traced here: 258 us
  Pallas kernels  170 us (66%)
  matrix products  45.9 us (18%)
  other arithmetic  30.6 us (12%)
  local copies, waits for them, and re-layouts  12.1 us (5%)
    pallas_call x1, Pallas kernels, rotate(): pl.pallas_call(functools.partial(rotate_kernel, n), out_shape=(jax.ShapeD...  160 us
    dot_general x1, matrix products, on_device(): jnp.einsum('qfd,qkd->qkf', precond, right_rows, preferred_element_type=jn...  45.9 us
    div x1, other arithmetic, on_device(): precond = (product / divisor[None]).astype(jnp.bfloat16)  18.7 us
    pallas_call x1, Pallas kernels, total(): pl.pallas_call(functools.partial(total_kernel, n, layers), out_shape=jax....  9.79 us
    gather x1, local copies, waits for them, and re-layouts, on_device(): jnp.take(in_whole, chosen, axis=0).reshape(NQ, WIN * R, features)  6.64 us
    select_n x2, other arithmetic, on_device(): jnp.take(in_whole, chosen, axis=0).reshape(NQ, WIN * R, features)  6.09 us

profile of v1, /device:TPU:0, one launch (start us, length us, event | category | flops | bytes accessed | tf_op | source)
XLA Modules:
  0.0 258.1 jit_solution(13407565793685863343)
XLA Ops:
  0.0 0.1 lt.41
  0.1 0.7 lt.42
  0.8 0.1 lt.43
  0.9 1.9 bitcast_multiply_fusion.mk_ref
  2.9 0.0 copy-start.3
  2.9 159.7 %shard_map.91 = (bf16[128,2048]{1,0:T(8,128)(2,1)}, bf16[8,128,512]{2,1,0:T(8,128)(2,1)}, bf16[8,64,4096]{2,1,0:T(8,128)(2,1)}, bf16[8,64,2048]{2,1,0:T(8,128)(2,1)}) custom-call(bf16[128,2048]{1,0:T(8,128)(2,1)} %bitcast.41, bf16[128,512]{1,0:T(8,128)(2,1)} %bitcast.42, bf16[64,4096]{1,0:T(8,128)(2,1)} %bitcast_multiply_fusion.mk_ref, ...), custom_call_target="tpu_custom_call" | custom-call | tf_op jit(solution)/shard_map/pallas_call | solution.py:279
  162.6 0.0 copy-done.3
  162.6 0.1 reshape.100
  162.7 0.0 copy-start.4
  162.7 6.6 %gather_fusion = bf16[24,32,4096]{2,1,0:T(8,128)(2,1)} fusion(bf16[16,32,4096]{2,1,0:T(8,128)(2,1)} %bitcast.35, s32[1024]{0:T(1024)S(1)} %pad_clamp_fusion), kind=kCustom, calls=%fused_computation | custom fusion | bytes 12583008 | tf_op jit(solution)/shard_map/jit(_take)/gather | solution.py:409
  169.3 0.0 copy-done.4
  169.3 0.1 broadcast_in_dim.28
  169.4 0.1 broadcast_in_dim.29
  169.5 0.0 copy-start.1
  169.5 0.0 copy-start
  169.5 6.1 %bitcast_select_fusion = bf16[4,192,4096]{2,1,0:T(8,128)(2,1)} fusion(pred[4,192]{1,0:T(4,128)(4,1)S(1)} %broadcast_in_dim.29, bf16[4,192,4096]{2,1,0:T(8,128)(2,1)} %bitcast.33), kind=kLoop, calls=%fused_computation.6 | loop fusion | flops 3145728 | bytes 12583680 | tf_op jit(solution)/shard_map/jit(_take)/select_n | solution.py:409
  175.6 0.0 copy-done.1
  175.6 0.0 copy-done
  175.6 0.6 copy.14
  176.2 0.5 reshape.103
  176.7 0.0 copy-start.5
  176.7 18.7 %add_bitcast_fusion = f32[2048,4096]{1,0:T(8,128)} fusion(bf16[1,2048,4096]{2,1,0:T(8,128)(2,1)} %param.13), kind=kLoop, calls=%fused_computation.4 | loop fusion | flops 16777216 | bytes 50331648 | tf_op jit(solution)/shard_map/div | solution.py:406
  195.5 0.0 copy-done.5
  195.5 45.9 %fusion = f32[4,192,2048]{2,1,0:T(8,128)} fusion(bf16[4,192,4096]{2,1,0:T(8,128)(2,1)} %bitcast_select_fusion, f32[2048,4096]{1,0:T(8,128)} %add_bitcast_fusion, bf16[4,32,2048]{2,1,0:T(8,128)(2,1)S(1)} %bitcast.43, bf16[4,32,4096]{2,1,0:T(8,128)(2,1)S(1)} %reshape.103), kind=kOutput, calls=%fused_computation.3 | convolution fusion | flops 15099494400 | bytes 47710208 | tf_op jit(solution)/shard_map/qfd,qkd->qkf/dot_general | solution.py:410
  241.4 0.0 copy-start.2
  241.4 2.5 gather_fusion.1
  243.9 0.0 copy-done.2
  243.9 3.8 %multiply_reduce_fusion.x_ref = f32[4,192]{1,0:T(4,128)S(1)} fusion(f32[4,192,2048]{2,1,0:T(8,128)} %fusion, pred[4,192]{1,0:T(4,128)(4,1)S(1)} %copy-done.2, bf16[4,192,2048]{2,1,0:T(8,128)(2,1)S(1)} %bitcast.34), kind=kLoop, calls=%fused_computation.7 | loop fusion | flops 6290688 | bytes 9441024 | tf_op jit(solution)/shard_map/reduce_sum | solution.py:411
  247.7 9.8 %shard_map.92 = f32[4,192]{1,0:T(4,128)S(1)} custom-call(f32[4,192]{1,0:T(4,128)S(1)} %multiply_reduce_fusion.x_ref), custom_call_target="tpu_custom_call" | custom-call | tf_op jit(solution)/shard_map/pallas_call | solution.py:362
  257.4 0.1 reshape.105
  257.5 0.6 copy.12
  (6 shorter events, 0.0 us)
Async XLA Ops:
  2.9 159.7 %copy-start.3 = (s32[4,6]{1,0:T(4,128)S(1)}, s32[4,6]{1,0:T(4,128)}, u32[]{:S(2)}) copy-start(s32[4,6]{1,0:T(4,128)} %param.17) | copy-start | bytes 292
  162.7 6.6 %copy-start.4 = (s32[1024]{0:T(1024)}, s32[1024]{0:T(1024)S(1)}, u32[]{:S(2)}) copy-start(s32[1024]{0:T(1024)S(1)} %pad_clamp_fusion) | copy-start | bytes 12292
  169.5 6.1 %copy-start.1 = (pred[4,192]{1,0:T(4,128)(4,1)}, pred[4,192]{1,0:T(4,128)(4,1)S(1)}, u32[]{:S(2)}) copy-start(pred[4,192]{1,0:T(4,128)(4,1)S(1)} %broadcast_in_dim.29) | copy-start | bytes 2308
  169.5 6.1 %copy-start = (bf16[8,128,512]{2,1,0:T(8,128)(2,1)S(1)}, bf16[8,128,512]{2,1,0:T(8,128)(2,1)}, u32[]{:S(2)}) copy-start(bf16[8,128,512]{2,1,0:T(8,128)(2,1)} %get-tuple-element.11) | copy-start | bytes 3145732
  176.7 18.7 %copy-start.5 = (bf16[128,2048]{1,0:T(8,128)(2,1)S(1)}, bf16[128,2048]{1,0:T(8,128)(2,1)}, u32[]{:S(2)}) copy-start(bf16[128,2048]{1,0:T(8,128)(2,1)} %get-tuple-element.10) | copy-start | bytes 1572868
  241.4 2.5 copy-start.2

commit v2 on v1

--- a/solution.py
+++ b/solution.py
@@ -13,6 +13,8 @@
 R = 32
 SPAN = 128
 COLS = 256
+TILE = 256
+SPAN_COLS = 1024
 BUFFERS = 3
 MESH = pl.DeviceIdType.MESH
 
@@ -105,13 +107,11 @@
     og_ref,
     ia_ref,
     mk_ref,
-    os_ref,
     ob_ref,
     ib_ref,
     to_ref,
     ti_ref,
     mk_all,
-    os_all,
     og_all,
     ia_all,
     ti_own,
@@ -128,8 +128,6 @@
     mk_recv,
     ti_send,
     ti_recv,
-    os_send,
-    os_recv,
 ):
     me = lax.axis_index("dp")
     nh = n // 2
@@ -150,11 +148,6 @@
         pltpu.make_async_copy(og_ref, og_all.at[me], local_sem.at[1]),
         pltpu.make_async_copy(ib_ref, ib_buf, local_sem.at[2]),
         pltpu.make_async_copy(mk_ref, mk_all.at[me], local_sem.at[3]),
-        pltpu.make_async_copy(
-            os_ref.at[:, pl.ds(pl.multiple_of(me * width, width), width)],
-            os_all.at[me],
-            local_sem.at[4],
-        ),
     ]
     for copy in locals_:
         copy.start()
@@ -175,17 +168,6 @@
     og = Gather(n, me, og_ref, og_all, og_send, og_recv)
     mk = Gather(n, me, mk_ref, mk_all, mk_send, mk_recv)
     ti = Gather(n, me, ti_own, ti_ref, ti_send, ti_recv)
-
-    def slices(d):
-        to = lax.rem(me + d, n)
-        return pltpu.make_async_remote_copy(
-            src_ref=os_ref.at[:, pl.ds(pl.multiple_of(to * width, width), width)],
-            dst_ref=os_all.at[me],
-            send_sem=os_send.at[d],
-            recv_sem=os_recv.at[me],
-            device_id={"dp": to},
-            device_id_type=MESH,
-        )
 
     def dots(low, high):
         def one(k, carry):
@@ -239,10 +221,6 @@
         mk.wave(w)
         ti.wave(w)
 
-    @pl.loop(1, n)
-    def _(d):
-        slices(d).start()
-
     dots(nh, n)
     to_ref[...] = acc[...].astype(to_ref.dtype)
     mk.finish()
@@ -251,21 +229,8 @@
     for gather in (ia, og, mk, ti):
         gather.drain()
 
-    @pl.loop(1, n)
-    def _(d):
-        slices(d).wait_send()
-        source = lax.rem(me + d, n)
-        pltpu.make_async_remote_copy(
-            src_ref=os_all.at[source],
-            dst_ref=os_all.at[source],
-            send_sem=os_send.at[0],
-            recv_sem=os_recv.at[source],
-            device_id={"dp": source},
-            device_id_type=MESH,
-        ).wait_recv()
-
-
-def rotate(n, og, ia, mk, out_store, out_basis, in_basis):
+
+def rotate(n, og, ia, mk, out_basis, in_basis):
     tokens, depth = og.shape
     in_depth = ia.shape[1]
     width, in_width = out_basis.shape[1], in_basis.shape[1]
@@ -282,10 +247,9 @@
             jax.ShapeDtypeStruct((tokens, width), dtype),
             jax.ShapeDtypeStruct((n, tokens, in_width), dtype),
             jax.ShapeDtypeStruct((n, rows, full), dtype),
-            jax.ShapeDtypeStruct((n, rows, width), dtype),
         ),
-        in_specs=[anywhere] * 6,
-        out_specs=(vmem,) * 4,
+        in_specs=[anywhere] * 5,
+        out_specs=(vmem,) * 3,
         scratch_shapes=[
             pltpu.VMEM((n, tokens, depth), dtype),
             pltpu.VMEM((n, tokens, in_depth), dtype),
@@ -303,17 +267,67 @@
             recvs,
             sends,
             recvs,
-            pltpu.SemaphoreType.DMA((n,)),
-            pltpu.SemaphoreType.DMA((n,)),
         ],
         compiler_params=pltpu.CompilerParams(
             collective_id=0, has_side_effects=True, vmem_limit_bytes=60 << 20
         ),
-    )(og, ia, mk, out_store, out_basis, in_basis)
-
-
-def total_kernel(n, layers, x_ref, out_ref, dp_slots, sub_total, layer_slots, local_sem, dp_send, dp_recv, layer_send, layer_recv):
+    )(og, ia, mk, out_basis, in_basis)
+
+
+def score_kernel(
+    n,
+    layers,
+    winners_ref,
+    to_ref,
+    ti_ref,
+    mk_ref,
+    eig_ref,
+    os_ref,
+    out_ref,
+    os_all,
+    ti_full,
+    rows,
+    eig_buf,
+    turned,
+    mapped,
+    lanes,
+    partial,
+    dp_slots,
+    sub_total,
+    layer_slots,
+    eig_sem,
+    local_sem,
+    os_send,
+    os_recv,
+    dp_send,
+    dp_recv,
+    layer_send,
+    layer_recv,
+):
     me, my_layer = lax.axis_index("dp"), lax.axis_index("layer")
+    width = to_ref.shape[1]
+    tiles = width // TILE
+    features = eig_ref.shape[1]
+    in_width = ti_ref.shape[2]
+    seqs = os_ref.shape[0]
+    winning = rows.shape[0]
+    span = min(SPAN_COLS, features)
+
+    def fetch(t, slot):
+        at = pl.ds(pl.multiple_of(t * TILE, TILE), TILE)
+        return pltpu.make_async_copy(eig_ref.at[at], eig_buf.at[slot], eig_sem.at[slot])
+
+    for t in range(min(2, tiles)):
+        fetch(t, t).start()
+
+    def block(j):
+        return pl.ds(pl.multiple_of(j * width, width), width)
+
+    own_slice = pltpu.make_async_copy(
+        os_ref.at[:, :, block(me)], os_all.at[pl.ds(me * seqs, seqs)], local_sem.at[0]
+    )
+    own_slice.start()
+
     barrier = pltpu.get_barrier_semaphore()
     for axis, size, at in (("dp", n, me), ("layer", layers, my_layer)):
 
@@ -325,8 +339,83 @@
 
     pl.semaphore_wait(barrier, n + layers - 2)
 
+    def slices(d, source):
+        to = lax.rem(me + d, n)
+        return pltpu.make_async_remote_copy(
+            src_ref=os_ref.at[:, :, block(to)],
+            dst_ref=os_all.at[pl.ds(source * seqs, seqs)],
+            send_sem=os_send.at[d],
+            recv_sem=os_recv.at[source],
+            device_id={"dp": to},
+            device_id_type=MESH,
+        )
+
+    @pl.loop(1, n)
+    def _(d):
+        slices(d, me).start()
+
+    for j in range(n):
+        ti_full[:, j * in_width : (j + 1) * in_width] = ti_ref[j]
+
+    @pl.loop(0, winning)
+    def _(i):
+        rows[i] = mk_ref[winners_ref[i]]
+
+    token = lax.broadcasted_iota(jnp.int32, (TILE, NQ * TQ), 1)
+
+    @pl.loop(0, tiles)
+    def _(t):
+        slot = lax.rem(t, 2)
+        fetch(t, slot).wait()
+        at = pl.ds(pl.multiple_of(t * TILE, TILE), TILE)
+        flipped = to_ref[:, at].astype(jnp.float32).T
+        for q in range(NQ):
+            mine = (token >= q * TQ) & (token < (q + 1) * TQ)
+            turned[q] = jnp.where(mine, flipped, 0.0).astype(turned.dtype)
+
+        def piece(c, carry):
+            cols = pl.ds(pl.multiple_of(c * span, span), span)
+            scale = 1.0 / (eig_buf[slot, :, cols].astype(jnp.float32) + damping)
+            for q in range(NQ):
+                product = jnp.dot(
+                    turned[q], ti_full[:, cols], preferred_element_type=jnp.float32
+                )
+                precond = (product * scale).astype(jnp.bfloat16)
+                right = rows[q * WIN : (q + 1) * WIN, :, cols].reshape(WIN * R, span)
+                part = lax.dot_general(
+                    right, precond, (((1,), (1,)), ((), ())), preferred_element_type=jnp.float32
+                )
+                mapped[t, q] = jnp.where(c == 0, part, mapped[t, q] + part)
+            return carry
+
+        lax.fori_loop(0, features // span, piece, 0)
+
+        @pl.when(t + 2 < tiles)
+        def _():
+            fetch(t + 2, slot).start()
+
+    own_slice.wait()
+
+    @pl.loop(1, n)
+    def _(d):
+        slices(d, me).wait_send()
+        slices(d, lax.rem(me + d, n)).wait_recv()
+
+    for i in range(winning):
+        q, w = divmod(i, WIN)
+        win = winners_ref[i]
+        summed = jnp.zeros((R, TILE), jnp.float32)
+        for t in range(tiles):
+            left = os_all[win, :, t * TILE : (t + 1) * TILE].astype(jnp.float32)
+            summed += mapped[t, q, w * R : (w + 1) * R, :] * left
+        folded = summed[:, :128]
+        for k in range(1, TILE // 128):
+            folded += summed[:, k * 128 : (k + 1) * 128]
+        lanes[i] = folded
+    partial[...] = jnp.sum(lanes[...], axis=2)
+
     def stage(axis, size, at, source, slots, send_sem, recv_sem):
-        own = pltpu.make_async_copy(source, slots.at[at], local_sem)
+        own = pltpu.make_async_copy(source, slots.at[at], local_sem.at[1])
         own.start()
 
         def push(d, slot):
@@ -353,31 +442,45 @@
             0, size, lambda i, total: total + slots[i], jnp.zeros(slots.shape[1:], slots.dtype)
         )
 
-    sub_total[...] = stage("dp", n, me, x_ref, dp_slots, dp_send, dp_recv)
+    sub_total[...] = stage("dp", n, me, partial, dp_slots, dp_send, dp_recv)
     out_ref[...] = stage("layer", layers, my_layer, sub_total, layer_slots, layer_send, layer_recv)
 
 
-def total(n, layers, x):
+def score(n, layers, winners, turned_out, turned_in, masked, eigenvalues, out_store):
+    tokens, width = turned_out.shape
+    features = eigenvalues.shape[1]
+    count = masked.shape[0]
+    winning = winners.shape[0]
+    small = (winning, R)
     vmem = pl.BlockSpec(memory_space=pltpu.VMEM)
+    anywhere = pl.BlockSpec(memory_space=pl.ANY)
+    dma = pltpu.SemaphoreType.DMA
     return pl.pallas_call(
-        functools.partial(total_kernel, n, layers),
-        out_shape=jax.ShapeDtypeStruct(x.shape, x.dtype),
-        in_specs=[vmem],
+        functools.partial(score_kernel, n, layers),
+        out_shape=jax.ShapeDtypeStruct(small, jnp.float32),
+        in_specs=[
+            pl.BlockSpec(memory_space=pltpu.SMEM), vmem, vmem, vmem, anywhere, anywhere
+        ],
         out_specs=vmem,
         scratch_shapes=[
-            pltpu.VMEM((n, *x.shape), x.dtype),
-            pltpu.VMEM(x.shape, x.dtype),
-            pltpu.VMEM((layers, *x.shape), x.dtype),
-            pltpu.SemaphoreType.DMA,
-            pltpu.SemaphoreType.DMA((n,)),
-            pltpu.SemaphoreType.DMA((n,)),
-            pltpu.SemaphoreType.DMA((layers,)),
-            pltpu.SemaphoreType.DMA((layers,)),
+            pltpu.VMEM((count, R, width), jnp.bfloat16),
+            pltpu.VMEM((tokens, features), jnp.bfloat16),
+            pltpu.VMEM((winning, R, features), jnp.bfloat16),
+            pltpu.VMEM((2, TILE, features), jnp.bfloat16),
+            pltpu.VMEM((NQ, TILE, tokens), jnp.bfloat16),
+            pltpu.VMEM((width // TILE, NQ, WIN * R, TILE), jnp.float32),
+            pltpu.VMEM((winning, R, 128), jnp.float32),
+            pltpu.VMEM(small, jnp.float32),
+            pltpu.VMEM((n, *small), jnp.float32),
+            pltpu.VMEM(small, jnp.float32),
+            pltpu.VMEM((layers, *small), jnp.float32),
+            dma((2,)), dma((2,)), dma((n,)), dma((n,)), dma((n,)), dma((n,)),
+            dma((layers,)), dma((layers,)),
         ],
         compiler_params=pltpu.CompilerParams(
-            collective_id=1, has_side_effects=True, vmem_limit_bytes=8 << 20
+            collective_id=1, has_side_effects=True, vmem_limit_bytes=60 << 20
         ),
-    )(x)
+    )(winners, turned_out, turned_in, masked, eigenvalues, out_store)
 
 
 def on_device(
@@ -385,31 +488,27 @@
     out_grads, in_acts, out_basis, in_basis, eigenvalues, out_store, in_store, counts, winners
 ):
     _, seqs, tokens, features = in_store.shape
-    width = out_basis.shape[2]
     alive = (jnp.arange(R, dtype=jnp.int32)[None, :] * SPAN < counts[:, None]).astype(jnp.bfloat16)
     masked = in_store[0] * alive[:, :, None]
-    turned_out, turned_in, in_whole, out_slices = rotate(
+    turned_out, turned_in, in_whole = rotate(
         n,
         out_grads[0],
         in_acts[0],
         masked.reshape(seqs * tokens, features),
-        out_store[0].reshape(seqs * tokens, out_store.shape[3]),
         out_basis[0],
         in_basis[0],
     )
-    in_whole = in_whole.reshape(n * seqs, tokens, features)
-    out_slices = out_slices.reshape(n * seqs, tokens, width)
-    left = turned_out.reshape(NQ, TQ, width)
-    right = turned_in.reshape(n, NQ, TQ, in_basis.shape[2]).transpose(1, 2, 0, 3).reshape(NQ, TQ, features)
-    product = jnp.einsum("qtf,qtd->qfd", left, right, preferred_element_type=jnp.float32)
-    divisor = eigenvalues[0].astype(jnp.float32) + damping
-    precond = (product / divisor[None]).astype(jnp.bfloat16)
-    chosen = winners.reshape(NQ * WIN)
-    left_rows = jnp.take(out_slices, chosen, axis=0).reshape(NQ, WIN * R, width)
-    right_rows = jnp.take(in_whole, chosen, axis=0).reshape(NQ, WIN * R, features)
-    mapped = jnp.einsum("qfd,qkd->qkf", precond, right_rows, preferred_element_type=jnp.float32)
-    partial_value = jnp.sum(mapped * left_rows.astype(jnp.float32), axis=2)
-    return total(n, layers, partial_value).reshape(NQ, WIN, R)
+    totals = score(
+        n,
+        layers,
+        winners.reshape(NQ * WIN),
+        turned_out,
+        turned_in,
+        in_whole.reshape(n * seqs, tokens, features),
+        eigenvalues[0],
+        out_store[0],
+    )
+    return totals.reshape(NQ, WIN, R)
 
 
 def solution(mesh):

time: 259 us -> 203 us (0.78)
  matrix products: 45.9 us -> 0 us
  other arithmetic: 30.6 us -> 1.96 us
  Pallas kernels: 170 us -> 198 us
  local copies, waits for them, and re-layouts: 12.1 us -> 2.81 us
    pallas_call x1, Pallas kernels: 9.79 us -> 62 us  [score(): pl.pallas_call(functools.partial(score_kernel, n, layers), out_shape=jax....]
    dot_general x1 -> x0, matrix products: 45.9 us -> none  [on_device(): jnp.einsum('qfd,qkd->qkf', precond, right_rows, preferred_element_type=jn...]
    pallas_call x1, Pallas kernels: 160 us -> 136 us  [rotate(): pl.pallas_call(functools.partial(rotate_kernel, n), out_shape=(jax.ShapeD...]
    div x1 -> x0, other arithmetic: 18.7 us -> none  [on_device(): precond = (product / divisor[None]).astype(jnp.bfloat16)]
    gather x2 -> x0, local copies, waits for them, and re-layouts: 9.1 us -> none  [the longest x1 6.64 us: on_device(): jnp.take(in_whole, chosen, axis=0).reshape(NQ, WIN * R, features)]
    select_n x2 -> x0, other arithmetic: 6.09 us -> none  [on_device(): jnp.take(in_whole, chosen, axis=0).reshape(NQ, WIN * R, features)]
    reduce_sum x1 -> x0, other arithmetic: 3.76 us -> none  [on_device(): partial_value = jnp.sum(mapped * left_rows.astype(jnp.float32), axis=2)]
where the time goes in v2:
time: 203 us
  Pallas kernels  198 us (98%)
  local copies, waits for them, and re-layouts  2.81 us (1%)
    pallas_call x1, Pallas kernels, rotate(): pl.pallas_call(functools.partial(rotate_kernel, n), out_shape=(jax.ShapeD...  136 us
    pallas_call x1, Pallas kernels, score(): pl.pallas_call(functools.partial(score_kernel, n, layers), out_shape=jax....  62 us

profile of v2, /device:TPU:0, one launch (start us, length us, event | category | flops | bytes accessed | tf_op | source)
XLA Modules:
  0.0 203.2 jit_solution(5397008905158009941)
XLA Ops:
  0.0 0.1 lt.22
  0.1 0.7 lt.23
  0.8 0.1 lt.24
  0.9 1.9 bitcast_multiply_fusion.mk_ref
  2.9 0.0 copy-start
  2.9 136.4 %shard_map.91 = (bf16[128,2048]{1,0:T(8,128)(2,1)}, bf16[8,128,512]{2,1,0:T(8,128)(2,1)}, bf16[8,64,4096]{2,1,0:T(8,128)(2,1)}) custom-call(bf16[128,2048]{1,0:T(8,128)(2,1)} %bitcast.15, bf16[128,512]{1,0:T(8,128)(2,1)} %bitcast.16, bf16[64,4096]{1,0:T(8,128)(2,1)} %bitcast_multiply_fusion.mk_ref, bf16[16384,2048]{1,0:T(8,128)(2,1)} %bitcast.3.ob_ref, ...), custom_call_target="tpu_custom_call" | custom-call | tf_op jit(solution)/shard_map/pallas_call | solution.py:244
  139.3 0.0 copy-done
  139.3 0.6 reshape.43.winners_ref
  139.9 62.0 %shard_map.92 = f32[24,32]{1,0:T(8,128)} custom-call(s32[24]{0:T(128)} %reshape.43.winners_ref, bf16[128,2048]{1,0:T(8,128)(2,1)} %get-tuple-element.8.to_ref, bf16[8,128,512]{2,1,0:T(8,128)(2,1)} %get-tuple-element.9.ti_ref, bf16[16,32,4096]{2,1,0:T(8,128)(2,1)} %bitcast.13, bf16[2048,4096]{1,0:T(8,128)(2,1)} %bitcast.11, bf16[2,32,16384]{2,1,0:T(8,128)(2,1)} %bitcast.14), custom_call_target="tpu_custom_call" | custom-call | tf_op jit(solution)/shard_map/pallas_call | solution.py:458
  201.9 0.7 reshape.45
  202.6 0.6 copy.11
  (3 shorter events, 0.0 us)
Async XLA Ops:
  2.9 136.4 %copy-start = (s32[4,6]{1,0:T(4,128)S(1)}, s32[4,6]{1,0:T(4,128)}, u32[]{:S(2)}) copy-start(s32[4,6]{1,0:T(4,128)} %param.17) | copy-start | bytes 292
